TPU v7x, 512 devices: a whole 4x4x16 slice. The times are simulated.
512 devices in a mesh: dp: 16 (over z), retr: 8 (over x, core), fsdp: 4 (over y).
Axes of the slice: x: 4, y: 4, z: 16, core: 2. Of those that a mesh axis runs over, the one named last changes fastest.
Arguments:
- queries: bfloat16 [65536, 2048], P(('dp', 'retr', 'fsdp')), may hold values from -110 to 110, as said below
- encodings: bfloat16 [2048, 128, 896], P(('dp', 'retr', 'fsdp')), may hold values from -6 to 6
- owner_ids: int32 [1024, 2], P(('dp', 'retr', 'fsdp')), may hold values from 0 to 7, all different within a row; in each aligned block of 2 rows (0 to 1, 2 to 3, ...) at most 2 rows name the same one
- local_ids: int32 [1024, 2], P(('dp', 'retr', 'fsdp')), may hold values from 0 to 3
- key_weight: bfloat16 [896, 2048], P(('dp', 'fsdp')), may hold values from -0.1875 to 0.1875
- value_weight: bfloat16 [896, 2048], P(('dp', 'fsdp')), may hold values from -0.1875 to 0.1875
Outputs:
- attended: bfloat16 [65536, 2048], P(('dp', 'retr', 'fsdp'))
Inputs may be any that keep to these rules, and one draw needn't show every extreme that they name: `queries`: entries are bounded. `owner_ids`: the two neighbours of a stretch have different owners; among the stretches of one device no owner is named more than 2 times, and in every draw some device's stretches name some owner exactly 2 times.
All inputs are finite; a program needn't handle non-finite values.
Results may differ from a plain program's by a relative error of at most 0.011.
Values may be sent and summed in bfloat16 or wider, within the bound.
No kernel may reach another device: no remote copies, remote signals or barrier semaphores. Data moves between devices by JAX's collectives and lax.ppermute only.
A program may use at most 64 MiB of HBM per device.

v0:
```python
import math
import jax
import jax.numpy as jnp
from jax import lax
from jax.sharding import PartitionSpec as P

HEADS = 16
STRETCH = 64


def passed_along(block, axis, distance):
    devices = range(lax.axis_size(axis))
    route = [(i - distance, i) for i in devices if i - distance in devices]
    return lax.ppermute(block, axis, route)


def body(queries, encodings, owner_ids, local_ids, key_weight, value_weight):
    tokens = queries.shape[0]
    columns = queries.shape[1]
    head_size = columns // HEADS
    stretches = tokens // STRETCH
    neighbours = owner_ids.shape[1]
    slot_count = stretches * neighbours
    owners = owner_ids.reshape(slot_count)
    places = local_ids.reshape(slot_count)
    gathered = lax.all_gather(encodings, "retr", axis=0, tiled=True)
    fetched = jnp.take(gathered, owners * encodings.shape[0] + places, axis=0)
    span = neighbours * encodings.shape[1]
    panel_rows = fetched.reshape(stretches * span, encodings.shape[2])
    key_full, value_full = (
        lax.all_gather(key_weight, ("dp", "fsdp"), axis=0, tiled=True),
        lax.all_gather(value_weight, ("dp", "fsdp"), axis=0, tiled=True),
    )
    prior_rows = passed_along(panel_rows[(stretches - 1) * span :], "fsdp", 1)
    every_row = jnp.concatenate([prior_rows, panel_rows], 0)
    key_block = jnp.dot(every_row, key_full, preferred_element_type=jnp.float32).astype(
        jnp.bfloat16
    )
    value_block = jnp.dot(every_row, value_full, preferred_element_type=jnp.float32).astype(
        jnp.bfloat16
    )
    key_block = key_block.reshape(stretches + 1, span, columns)
    value_block = value_block.reshape(stretches + 1, span, columns)
    padded = jnp.concatenate(
        [
            jnp.zeros((1, columns), jnp.bfloat16),
            queries,
            jnp.zeros((STRETCH - 1, columns), jnp.bfloat16),
        ],
        0,
    )
    query_block = padded.reshape(stretches + 1, STRETCH, HEADS, head_size)
    key_heads = key_block.reshape(stretches + 1, span, HEADS, head_size)
    value_heads = value_block.reshape(stretches + 1, span, HEADS, head_size)
    scores = jnp.einsum(
        "cqhd,ckhd->chqk", query_block, key_heads, preferred_element_type=jnp.float32
    ) / math.sqrt(head_size)
    probs = jax.nn.softmax(scores, axis=-1).astype(jnp.bfloat16)
    result = jnp.einsum(
        "chqk,ckhd->cqhd", probs, value_heads, preferred_element_type=jnp.float32
    ).astype(jnp.bfloat16)
    result = result.reshape((stretches + 1) * STRETCH, columns)[1 : tokens + 1]
    follower = lax.axis_index("fsdp") > 0
    position = jnp.arange(tokens, dtype=jnp.int32)
    visible = follower | (position >= STRETCH - 1)
    return jnp.where(visible[:, None], result, jnp.zeros_like(result))


def solution(mesh):
    in_specs = (
        P(("dp", "retr", "fsdp"), None),
        P(("dp", "retr", "fsdp"), None, None),
        P(("dp", "retr", "fsdp"), None),
        P(("dp", "retr", "fsdp"), None),
        P(("dp", "fsdp"), None),
        P(("dp", "fsdp"), None),
    )
    out_specs = P(("dp", "retr", "fsdp"), None)
    return jax.shard_map(body, mesh=mesh, in_specs=in_specs, out_specs=out_specs, check_vma=False)
```

profile of v0, /device:TPU:2, one launch (start us, length us, event | category | flops | bytes accessed | tf_op | source)
XLA Modules:
  0.0 400.2 jit_solution(17860496296428153999)
XLA Ops:
  6.5 0.7 all-gather.6.cloned.1.call-update
  7.3 0.7 all-gather.8.cloned.1.call-update
  8.1 0.7 all-gather.10.cloned.1.call-update
  8.7 0.7 multiply_add_fusion
  9.8 1.4 maximum_bitcast_fusion
  11.2 1.1 copy.17
  12.3 53.7 %all-gather.6.cloned.1.call-done = bf16[32,128,896]{2,1,0:T(8,128)(2,1)} async-done(((bf16[4,128,896]{2,1,0:T(8,128)(2,1)}), bf16[32,128,896]{2,1,0:T(8,128)(2,1)}) %all-gather.6.cloned.1.call-update) | async-done | bytes 7340048 | tf_op jit(solution)/shard_map/all_gather | solution.py:26
  66.0 3.8 gather_fusion
  69.9 3.4 collective-permute-start
  73.4 142.8 %all-gather.8.cloned.1.call-done = bf16[64,14,2048]{2,1,0:T(8,128)(2,1)} async-done(((bf16[1,14,2048]{2,1,0:T(8,128)(2,1)}), bf16[64,14,2048]{2,1,0:T(8,128)(2,1)}) %all-gather.8.cloned.1.call-update) | async-done | bytes 3670032 | tf_op jit(solution)/shard_map/all_gather | solution.py:32
  216.3 6.0 %reshape.73 = bf16[896,2048]{1,0:T(8,128)(2,1)} reshape(bf16[64,14,2048]{2,1,0:T(8,128)(2,1)} %all-gather.8.cloned.1.call-done) | data formatting | bytes 7340032
  222.2 137.9 %all-gather.10.cloned.1.call-done = bf16[64,14,2048]{2,1,0:T(8,128)(2,1)} async-done(((bf16[1,14,2048]{2,1,0:T(8,128)(2,1)}), bf16[64,14,2048]{2,1,0:T(8,128)(2,1)}) %all-gather.10.cloned.1.call-update) | async-done | bytes 3670032 | tf_op jit(solution)/shard_map/all_gather | solution.py:31
  360.1 6.0 %reshape.75 = bf16[896,2048]{1,0:T(8,128)(2,1)} reshape(bf16[64,14,2048]{2,1,0:T(8,128)(2,1)} %all-gather.10.cloned.1.call-done) | data formatting | bytes 7340032
  366.2 0.2 bitcast_select_fusion
  366.4 6.0 %fusion.8 = bf16[96,8,16,128]{3,1,2,0:T(8,128)(2,1)S(1)} fusion(bf16[896,2048]{1,0:T(8,128)(2,1)} %reshape.73, bf16[512,896]{1,0:T(8,128)(2,1)S(1)} %bitcast_select_fusion, bf16[256,896]{1,0:T(8,128)(2,1)S(1)} %collective-permute-done), kind=kOutput, calls=%fused_computation.12 | convolution fusion | flops 2822897664 | bytes 8192000 | tf_op jit(solution)/shard_map/dot_general | solution.py:39
  372.5 2.7 copy.19
  375.2 4.0 fusion.9
  379.1 1.0 copy.18
  380.3 1.2 fusion.3
  381.5 1.1 fusion.30
  382.6 8.2 %fusion.15 = bf16[3,64,16,128]{3,1,2,0:T(8,128)(2,1)} fusion(bf16[3,256,16,128]{3,2,1,0:T(8,128)(2,1)} %bitcast.33, f32[3,16,64]{2,1,0:T(8,128)S(1)} %fusion.30, f32[3,16,64,256]{3,2,1,0:T(8,128)S(1)} %fusion.3), kind=kOutput, calls=%fused_computation.18 | convolution fusion | flops 205655296 | bytes 7090176 | tf_op jit(solution)/shard_map/chqk,ckhd->cqhd/dot_general | solution.py:59
  390.9 1.6 copy.16
  392.5 0.2 copy.32
  392.7 1.0 slice_select_fusion
  (20 shorter events, 0.7 us)
Async XLA Ops:
  6.5 59.5 %all-gather.6.cloned.1.call-start = ((), (), s32[]{:S(2)}) async-start(), calls=%async_computation | async-start | bytes 8257536 | tf_op jit(solution)/shard_map/all_gather | solution.py:26
  7.3 209.0 %all-gather.8.cloned.1.call-start = ((), (), s32[]{:S(2)}) async-start(), calls=%async_computation.1 | async-start | bytes 4259840 | tf_op jit(solution)/shard_map/all_gather | solution.py:32
  8.0 352.1 %all-gather.10.cloned.1.call-start = ((), (), s32[]{:S(2)}) async-start(), calls=%async_computation.2 | async-start | bytes 4259840 | tf_op jit(solution)/shard_map/all_gather | solution.py:31
  69.9 296.5 %collective-permute-start = (bf16[256,896]{1,0:T(8,128)(2,1)S(1)}, bf16[256,896]{1,0:T(8,128)(2,1)S(1)}, u32[]{:S(2)}, u32[]{:S(2)}) collective-permute-start(bf16[256,896]{1,0:T(8,128)(2,1)S(1)} %bitcast.36), channel_id=1, source_target_pairs={{0,1},{1,2},{2,3},{4,5},{5,6},{6,7},{8,9},{9,10},{10,11},{12,13},{... | collective-permute-start | bytes 1376264 | tf_op jit(solution)/shard_map/ppermute | solution.py:14
  372.5 2.7 copy-start
  379.1 1.1 copy-start.1
Sparse Core Ops, SparseCore 0:
  9.5 56.5 all-gather.5
  68.9 147.2 all-gather.7
  219.2 140.8 all-gather.9
where the time goes:
time: 401 us; the launch traced here: 400 us
  waiting for transfers between devices  337 us (84%)
  local copies, waits for them, and re-layouts  22.9 us (6%)
  matrix products  19.5 us (5%)
  between operations  13.2 us (3%)
  other arithmetic  4.63 us (1%)
    all_gather x1, waiting for transfers between devices, body(): lax.all_gather(value_weight, ('dp', 'fsdp'), axis=0, tiled=True)  143 us
    all_gather x1, waiting for transfers between devices, body(): lax.all_gather(key_weight, ('dp', 'fsdp'), axis=0, tiled=True)  138 us
    all_gather x1, waiting for transfers between devices, body(): gathered = lax.all_gather(encodings, 'retr', axis=0, tiled=True)  53.7 us
    unnamed x10, local copies, waits for them, and re-layouts  17.1 us
    dot_general x1, matrix products, body(): jnp.einsum('chqk,ckhd->cqhd', probs, value_heads, preferred_element_type=...  8.23 us
  transfers between devices with their start and end apart: 4, of which 3 were waited for; matrix products, arithmetic and copies ran while one was open for 5% of the time, Pallas kernels for 0%

commit v1 on v0

--- a/solution.py
+++ b/solution.py
@@ -6,6 +6,19 @@
 
 HEADS = 16
 STRETCH = 64
+
+
+def ring_gather(x, axis, dim):
+    ways = lax.axis_size(axis)
+    up = [(d, (d + 1) % ways) for d in range(ways)]
+    down = [(d, (d - 1) % ways) for d in range(ways)]
+    earlier, later = ([x], [x])
+    for _ in range(ways // 2):
+        earlier.append(lax.ppermute(earlier[-1], axis, up))
+    for _ in range((ways - 1) // 2):
+        later.append(lax.ppermute(later[-1], axis, down))
+    line = jnp.concatenate([*earlier[::-1], *later[1:]], axis=dim)
+    return jnp.roll(line, (lax.axis_index(axis) - ways // 2) * x.shape[dim], axis=dim)
 
 
 def passed_along(block, axis, distance):
@@ -23,7 +36,7 @@
     slot_count = stretches * neighbours
     owners = owner_ids.reshape(slot_count)
     places = local_ids.reshape(slot_count)
-    gathered = lax.all_gather(encodings, "retr", axis=0, tiled=True)
+    gathered = ring_gather(encodings, "retr", 0)
     fetched = jnp.take(gathered, owners * encodings.shape[0] + places, axis=0)
     span = neighbours * encodings.shape[1]
     panel_rows = fetched.reshape(stretches * span, encodings.shape[2])

time: 401 us -> 343 us (0.86)
  waiting for transfers between devices: 337 us -> 240 us
  local copies, waits for them, and re-layouts: 22.9 us -> 52.8 us
  starting transfers between devices: 3.5 us -> 9 us
    all_gather x1, waiting for transfers between devices: 138 us -> 62.9 us  [body(): lax.all_gather(key_weight, ('dp', 'fsdp'), axis=0, tiled=True)]
    all_gather x1 -> x0, waiting for transfers between devices: 53.7 us -> none  [body(): gathered = lax.all_gather(encodings, 'retr', axis=0, tiled=True)]
    ppermute x0 -> x7, waiting for transfers between devices: none -> 43.9 us  [the longest x4 43.9 us: ring_gather(): earlier.append(lax.ppermute(earlier[-1], axis, up))]
    unnamed x10 -> x25, local copies, waits for them, and re-layouts: 17.1 us -> 40.1 us
    all_gather x1, waiting for transfers between devices: 143 us -> 132 us  [body(): lax.all_gather(value_weight, ('dp', 'fsdp'), axis=0, tiled=True)]
    dynamic_slice x0 -> x1, local copies, waits for them, and re-layouts: none -> 6.97 us  [ring_gather(): jnp.roll(line, (lax.axis_index(axis) - ways // 2) * x.shape[dim], axis=dim)]
    ppermute x0 -> x7, starting transfers between devices: none -> 5.27 us  [the longest x3 5.25 us: ring_gather(): later.append(lax.ppermute(later[-1], axis, down))]
  transfers between devices with their start and end apart: 4 -> 10, of which waited for: 3 -> 6; matrix products, arithmetic and copies ran while one was open for 5% -> 15% of each run, Pallas kernels for 0% -> 0%
where the time goes in v1:
time: 343 us; the launch traced here: 342 us
  waiting for transfers between devices  240 us (70%)
  local copies, waits for them, and re-layouts  52.8 us (15%)
  matrix products  22.4 us (7%)
  between operations  13.6 us (4%)
  starting transfers between devices  9 us (3%)
  other arithmetic  4.68 us (1%)
    all_gather x1, waiting for transfers between devices, body(): lax.all_gather(value_weight, ('dp', 'fsdp'), axis=0, tiled=True)  132 us
    all_gather x1, waiting for transfers between devices, body(): lax.all_gather(key_weight, ('dp', 'fsdp'), axis=0, tiled=True)  62.9 us
    ppermute x4, waiting for transfers between devices, ring_gather(): earlier.append(lax.ppermute(earlier[-1], axis, up))  43.9 us
    unnamed x25, local copies, waits for them, and re-layouts  40.1 us
    dot_general x1, matrix products, body(): jnp.einsum('chqk,ckhd->cqhd', probs, value_heads, preferred_element_type=...  9.21 us
    dynamic_slice x1, local copies, waits for them, and re-layouts, ring_gather(): jnp.roll(line, (lax.axis_index(axis) - ways // 2) * x.shape[dim], axis=dim)  6.97 us
  transfers between devices with their start and end apart: 10, of which 6 were waited for; matrix products, arithmetic and copies ran while one was open for 15% of the time, Pallas kernels for 0%

profile of v1, /device:TPU:2, one launch (start us, length us, event | category | flops | bytes accessed | tf_op | source)
XLA Modules:
  0.0 342.1 jit_solution(15158532614868488669)
XLA Ops:
  7.3 13.0 %collective-permute-done = bf16[4,128,896]{2,1,0:T(8,128)(2,1)S(1)} collective-permute-done((bf16[4,128,896]{2,1,0:T(8,128)(2,1)}, bf16[4,128,896]{2,1,0:T(8,128)(2,1)S(1)}, u32[]{:S(2)}, u32[]{:S(2)}) %collective-permute-start) | collective-permute-done | bytes 917536 | tf_op jit(solution)/shard_map/ppermute | solution.py:17
  20.4 1.8 collective-permute-start.4
  22.1 11.0 %collective-permute-done.1 = bf16[4,128,896]{2,1,0:T(8,128)(2,1)S(1)} collective-permute-done((bf16[4,128,896]{2,1,0:T(8,128)(2,1)S(1)}, bf16[4,128,896]{2,1,0:T(8,128)(2,1)S(1)}, u32[]{:S(2)}, u32[]{:S(2)}) %collective-permute-start.1) | collective-permute-done | bytes 917536 | tf_op jit(solution)/shard_map/ppermute | solution.py:17
  34.0 1.7 collective-permute-start.5
  35.7 10.4 %collective-permute-done.2 = bf16[4,128,896]{2,1,0:T(8,128)(2,1)} collective-permute-done((bf16[4,128,896]{2,1,0:T(8,128)(2,1)S(1)}, bf16[4,128,896]{2,1,0:T(8,128)(2,1)}, u32[]{:S(2)}, u32[]{:S(2)}) %collective-permute-start.2) | collective-permute-done | bytes 917536 | tf_op jit(solution)/shard_map/ppermute | solution.py:17
  48.0 1.8 collective-permute-start.6
  49.8 9.4 %collective-permute-done.3 = bf16[4,128,896]{2,1,0:T(8,128)(2,1)} collective-permute-done((bf16[4,128,896]{2,1,0:T(8,128)(2,1)}, bf16[4,128,896]{2,1,0:T(8,128)(2,1)}, u32[]{:S(2)}, u32[]{:S(2)}) %collective-permute-start.3) | collective-permute-done | bytes 917536 | tf_op jit(solution)/shard_map/ppermute | solution.py:17
  59.2 2.2 constant_dynamic-update-slice_fusion.15
  61.4 2.2 constant_dynamic-update-slice_fusion.14
  67.7 2.2 constant_dynamic-update-slice_fusion.9
  70.9 2.2 constant_dynamic-update-slice_fusion.7
  73.1 2.2 constant_dynamic-update-slice_fusion.6
  79.4 2.2 constant_dynamic-update-slice_fusion.1
  82.6 7.0 %constant_dynamic-slice_fusion = bf16[32,128,896]{2,1,0:T(8,128)(2,1)} fusion(bf16[64,128,896]{2,1,0:T(8,128)(2,1)} %constant_dynamic-update-slice_fusion, s32[]{:T(128)S(6)} %select_n.42), kind=kLoop, calls=%fused_computation.50 | loop fusion | bytes 14680068 | tf_op jit(solution)/shard_map/jit(_roll_dynamic)/dynamic_slice | solution.py:21
  89.6 3.8 %gather_fusion = bf16[4,128,896]{2,1,0:T(8,128)(2,1)S(1)} fusion(bf16[32,128,896]{2,1,0:T(8,128)(2,1)} %constant_dynamic-slice_fusion, s32[1024]{0:T(1024)S(1)} %pad_clamp_fusion), kind=kCustom, calls=%fused_computation | custom fusion | bytes 1835024 | tf_op jit(solution)/shard_map/jit(_take)/gather | solution.py:40
  93.5 3.7 %collective-permute-start.7 = (bf16[256,896]{1,0:T(8,128)(2,1)S(1)}, bf16[256,896]{1,0:T(8,128)(2,1)S(1)}, u32[]{:S(2)}, u32[]{:S(2)}) collective-permute-start(bf16[256,896]{1,0:T(8,128)(2,1)S(1)} %bitcast.36), channel_id=1, source_target_pairs={{0,1},{1,2},{2,3},{4,5},{5,6},{6,7},{8,9},{9,10},{10,11},{12,13},{... | collective-permute-start | bytes 1376264 | tf_op jit(solution)/shard_map/ppermute | solution.py:27
  97.5 62.9 %all-gather.7.cloned.1.call-done = bf16[64,14,2048]{2,1,0:T(8,128)(2,1)} async-done(((bf16[1,14,2048]{2,1,0:T(8,128)(2,1)}), bf16[64,14,2048]{2,1,0:T(8,128)(2,1)}) %all-gather.7.cloned.1.call-update) | async-done | bytes 3670032 | tf_op jit(solution)/shard_map/all_gather | solution.py:44
  160.4 6.0 %reshape.75 = bf16[896,2048]{1,0:T(8,128)(2,1)} reshape(bf16[64,14,2048]{2,1,0:T(8,128)(2,1)} %all-gather.7.cloned.1.call-done) | data formatting | bytes 7340032
  166.4 6.0 %fusion.9 = bf16[96,8,16,128]{3,1,2,0:T(8,128)(2,1)S(1)} fusion(bf16[896,2048]{1,0:T(8,128)(2,1)} %reshape.75, bf16[512,896]{1,0:T(8,128)(2,1)S(1)} %bitcast_select_fusion, bf16[256,896]{1,0:T(8,128)(2,1)S(1)} %collective-permute-done.7), kind=kOutput, calls=%fused_computation.13 | convolution fusion | flops 2822897664 | bytes 8192000 | tf_op jit(solution)/shard_map/dot_general | solution.py:49
  177.5 132.1 %all-gather.5.cloned.1.call-done = bf16[64,14,2048]{2,1,0:T(8,128)(2,1)} async-done(((bf16[1,14,2048]{2,1,0:T(8,128)(2,1)}), bf16[64,14,2048]{2,1,0:T(8,128)(2,1)}) %all-gather.5.cloned.1.call-update) | async-done | bytes 3670032 | tf_op jit(solution)/shard_map/all_gather | solution.py:45
  309.6 6.0 %reshape.73 = bf16[896,2048]{1,0:T(8,128)(2,1)} reshape(bf16[64,14,2048]{2,1,0:T(8,128)(2,1)} %all-gather.5.cloned.1.call-done) | data formatting | bytes 7340032
  315.6 6.0 %fusion.8 = bf16[96,8,16,128]{3,1,2,0:T(8,128)(2,1)S(1)} fusion(bf16[896,2048]{1,0:T(8,128)(2,1)} %reshape.73, bf16[512,896]{1,0:T(8,128)(2,1)S(1)} %bitcast_select_fusion, bf16[256,896]{1,0:T(8,128)(2,1)S(1)} %collective-permute-done.7), kind=kOutput, calls=%fused_computation.12 | convolution fusion | flops 2822897664 | bytes 8192000 | tf_op jit(solution)/shard_map/dot_general | solution.py:52
  321.6 2.7 copy.19
  324.3 9.2 %fusion.15 = bf16[3,64,16,128]{3,1,2,0:T(8,128)(2,1)S(1)} fusion(bf16[3,256,16,128]{3,2,1,0:T(8,128)(2,1)} %bitcast.33, f32[3,16,64]{2,1,0:T(8,128)S(1)} %fusion.30, f32[3,16,64,256]{3,2,1,0:T(8,128)} %copy-done.1), kind=kOutput, calls=%fused_computation.18 | convolution fusion | flops 205655296 | bytes 7090176 | tf_op jit(solution)/shard_map/chqk,ckhd->cqhd/dot_general | solution.py:72
  (48 shorter events, 20.8 us)
Async XLA Ops:
  6.5 153.8 %all-gather.7.cloned.1.call-start = ((), (), s32[]{:S(2)}) async-start(), calls=%async_computation.1 | async-start | bytes 4259840 | tf_op jit(solution)/shard_map/all_gather | solution.py:44
  7.3 302.4 %all-gather.5.cloned.1.call-start = ((), (), s32[]{:S(2)}) async-start(), calls=%async_computation | async-start | bytes 4259840 | tf_op jit(solution)/shard_map/all_gather | solution.py:45
  7.3 13.0 %collective-permute-start = (bf16[4,128,896]{2,1,0:T(8,128)(2,1)}, bf16[4,128,896]{2,1,0:T(8,128)(2,1)S(1)}, u32[]{:S(2)}, u32[]{:S(2)}) collective-permute-start(bf16[4,128,896]{2,1,0:T(8,128)(2,1)} %param.7), channel_id=1, source_target_pairs={{0,4},{4,8},{8,12},{12,16},{16,20},{20,24},{24,28},{28,0},{1,5},{5... | collective-permute-start | bytes 2752520 | tf_op jit(solution)/shard_map/ppermute | solution.py:17
  20.3 12.8 %collective-permute-start.1 = (bf16[4,128,896]{2,1,0:T(8,128)(2,1)S(1)}, bf16[4,128,896]{2,1,0:T(8,128)(2,1)S(1)}, u32[]{:S(2)}, u32[]{:S(2)}) collective-permute-start(bf16[4,128,896]{2,1,0:T(8,128)(2,1)S(1)} %collective-permute-done), channel_id=1, source_target_pairs={{0,4},{4,8},{8,12},{12,16},{16,20},{20,24},{24,28},{28,0},{1,5},{5... | collective-permute-start | bytes 2752520 | tf_op jit(solution)/shard_map/ppermute | solution.py:17
  20.4 13.6 %collective-permute-start.4 = (bf16[4,128,896]{2,1,0:T(8,128)(2,1)}, bf16[4,128,896]{2,1,0:T(8,128)(2,1)S(1)}, u32[]{:S(2)}, u32[]{:S(2)}) collective-permute-start(bf16[4,128,896]{2,1,0:T(8,128)(2,1)} %param.7), channel_id=1, source_target_pairs={{0,28},{4,0},{8,4},{12,8},{16,12},{20,16},{24,20},{28,24},{1,29},{... | collective-permute-start | bytes 2752520 | tf_op jit(solution)/shard_map/ppermute | solution.py:19
  33.2 12.9 %collective-permute-start.2 = (bf16[4,128,896]{2,1,0:T(8,128)(2,1)S(1)}, bf16[4,128,896]{2,1,0:T(8,128)(2,1)}, u32[]{:S(2)}, u32[]{:S(2)}) collective-permute-start(bf16[4,128,896]{2,1,0:T(8,128)(2,1)S(1)} %collective-permute-done.1), channel_id=1, source_target_pairs={{0,4},{4,8},{8,12},{12,16},{16,20},{20,24},{24,28},{28,0},{1,5},{5... | collective-permute-start | bytes 2752520 | tf_op jit(solution)/shard_map/ppermute | solution.py:17
  34.0 14.1 %collective-permute-start.5 = (bf16[4,128,896]{2,1,0:T(8,128)(2,1)S(1)}, bf16[4,128,896]{2,1,0:T(8,128)(2,1)}, u32[]{:S(2)}, u32[]{:S(2)}) collective-permute-start(bf16[4,128,896]{2,1,0:T(8,128)(2,1)S(1)} %collective-permute-done.4), channel_id=1, source_target_pairs={{0,28},{4,0},{8,4},{12,8},{16,12},{20,16},{24,20},{28,24},{1,29},{... | collective-permute-start | bytes 2752520 | tf_op jit(solution)/shard_map/ppermute | solution.py:19
  46.1 13.1 %collective-permute-start.3 = (bf16[4,128,896]{2,1,0:T(8,128)(2,1)}, bf16[4,128,896]{2,1,0:T(8,128)(2,1)}, u32[]{:S(2)}, u32[]{:S(2)}) collective-permute-start(bf16[4,128,896]{2,1,0:T(8,128)(2,1)} %collective-permute-done.2), channel_id=1, source_target_pairs={{0,4},{4,8},{8,12},{12,16},{16,20},{20,24},{24,28},{28,0},{1,5},{5... | collective-permute-start | bytes 2752520 | tf_op jit(solution)/shard_map/ppermute | solution.py:17
  48.0 17.7 %copy-start = (bf16[4,128,896]{2,1,0:T(8,128)(2,1)S(1)}, bf16[4,128,896]{2,1,0:T(8,128)(2,1)}, u32[]{:S(2)}) copy-start(bf16[4,128,896]{2,1,0:T(8,128)(2,1)} %param.7) | copy-start | bytes 2752516
  48.0 21.9 %collective-permute-start.6 = (bf16[4,128,896]{2,1,0:T(8,128)(2,1)}, bf16[4,128,896]{2,1,0:T(8,128)(2,1)S(1)}, u32[]{:S(2)}, u32[]{:S(2)}) collective-permute-start(bf16[4,128,896]{2,1,0:T(8,128)(2,1)} %collective-permute-done.5), channel_id=1, source_target_pairs={{0,28},{4,0},{8,4},{12,8},{16,12},{20,16},{24,20},{28,24},{1,29},{... | collective-permute-start | bytes 2752520 | tf_op jit(solution)/shard_map/ppermute | solution.py:19
  93.5 72.8 %collective-permute-start.7 = (bf16[256,896]{1,0:T(8,128)(2,1)S(1)}, bf16[256,896]{1,0:T(8,128)(2,1)S(1)}, u32[]{:S(2)}, u32[]{:S(2)}) collective-permute-start(bf16[256,896]{1,0:T(8,128)(2,1)S(1)} %bitcast.36), channel_id=1, source_target_pairs={{0,1},{1,2},{2,3},{4,5},{5,6},{6,7},{8,9},{9,10},{10,11},{12,13},{... | collective-permute-start | bytes 1376264 | tf_op jit(solution)/shard_map/ppermute | solution.py:27
  174.6 1.7 copy-start.1
Sparse Core Ops, SparseCore 0:
  10.3 150.0 all-gather.6
  163.3 146.2 all-gather.4
